TPU v7x, 256 devices: a whole 4x4x8 slice. The times are simulated.
256 devices in a mesh: sky: 32 (over y, z_lo, core), loop: 8 (over x, z_hi).
Axes of the slice: x: 4, y: 4, z: 8 (z_hi: 2, z_lo: 4; z = z_hi * 4 + z_lo), core: 2. Of those that a mesh axis runs over, the one named last changes fastest.
Arguments:
- queries: bfloat16 [196608, 256], P(('sky', 'loop')), may hold values from -1 to 1
- keys: bfloat16 [196608, 256], P(('sky', 'loop')), may hold values from -1 to 1
- partner_owner: int32 [196608, 4], P(('sky', 'loop')), may hold values from 0 to 31, as said below
- partner_row: int32 [196608, 4], P(('sky', 'loop')), may hold values from 0 to 767
- partner_count: int32 [196608], P(('sky', 'loop')), may hold values from 1 to 4, as said below
Outputs:
- loss: float32 [196608], P(('sky', 'loop'))
- grad_queries: float32 [196608, 256], P(('sky', 'loop'))
- grad_keys: float32 [196608, 256], P(('sky', 'loop'))
Inputs may be any that keep to these rules, and one draw needn't show every extreme that they name: `partner_owner`: each row names 4 different sky indices, never its own device's sky index; among the rows of one device no index is named more than 192 times, and on every device some index is named exactly 192 times. `partner_count`: some anchor has 4 live partners and some has one.
All inputs are finite; a program needn't handle non-finite values.
Results may differ from a plain program's by a relative error of at most 0.004.
Values may be sent and summed in bfloat16 or wider, within the bound.
A program may use at most 64 MiB of HBM per device.

v0:
```python
import jax
import jax.numpy as jnp
from jax import lax
from jax.sharding import PartitionSpec as P

SCALE = 10.0
EPS = 1e-06


def unit_rows(rows):
    wide = rows.astype(jnp.float32)
    norms = jnp.sqrt(jnp.sum(wide * wide, axis=1, keepdims=True) + EPS)
    return (wide / norms, norms)


def back_unit(unit, norms, grad):
    return (grad - unit * jnp.sum(unit * grad, axis=1, keepdims=True)) / norms


def fold_blocks(carry, pieces, step):
    total_rows = pieces[0].shape[0]
    size = 512
    number = total_rows // size
    split = tuple((piece.reshape((number, size) + piece.shape[1:]) for piece in pieces))
    offsets = size * jnp.arange(number, dtype=jnp.int32)

    def one_turn(summed, item):
        return (step(summed, item[0], item[1]), None)

    result, unused = lax.scan(one_turn, carry, (split, offsets))
    return result


def shards(queries, keys, partner_owner, partner_row, partner_count):
    anchors, width = queries.shape
    slots = partner_owner.shape[1]
    sky_count = lax.axis_size("sky")
    bucket = 2 * anchors * slots // sky_count
    unit_q, norm_q = unit_rows(queries)
    unit_k, norm_k = unit_rows(keys)
    query_rows = unit_q.astype(jnp.bfloat16)
    key_rows = unit_k.astype(jnp.bfloat16)
    mine = lax.axis_index("loop") * anchors + jnp.arange(anchors, dtype=jnp.int32)
    valid = jnp.arange(slots, dtype=jnp.int32)[None, :] < partner_count[:, None]
    inverse = 1.0 / (1.0 + partner_count.astype(jnp.float32))
    flat_owner = partner_owner.reshape(-1)
    owner_hits = (flat_owner[:, None] == jnp.arange(sky_count, dtype=jnp.int32)[None, :]).astype(
        jnp.int32
    )
    earlier = jnp.sum((jnp.cumsum(owner_hits, axis=0) - owner_hits) * owner_hits, axis=1)
    slot_index = flat_owner * bucket + earlier
    requests = (
        jnp.zeros((sky_count * bucket,), jnp.int32).at[slot_index].set(partner_row.reshape(-1))
    )
    incoming = lax.all_to_all(
        requests.reshape(sky_count, bucket), "sky", split_axis=0, concat_axis=0, tiled=True
    )
    wanted = incoming.reshape(-1)
    replies = jnp.take(key_rows, wanted, axis=0)
    answered = lax.all_to_all(
        replies.reshape(sky_count, bucket, width), "sky", split_axis=0, concat_axis=0, tiled=True
    )
    partner_keys = jnp.take(answered.reshape(-1, width), slot_index, axis=0).reshape(
        anchors, slots, width
    )
    outgoing = (
        jnp.zeros((sky_count * bucket, width), jnp.bfloat16)
        .at[slot_index]
        .set(jnp.repeat(query_rows, slots, axis=0))
    )
    partner_logits = SCALE * jnp.einsum(
        "apd,ad->ap", partner_keys, query_rows, preferred_element_type=jnp.float32
    )

    def add_exp(total, block, offset):
        scores = SCALE * jnp.dot(query_rows, block[0].T, preferred_element_type=jnp.float32)
        return total + jnp.sum(jnp.exp(scores), axis=1)

    start_sum = jnp.zeros((anchors,), jnp.float32)
    group_keys = lax.all_gather(key_rows, "loop", axis=0, tiled=True)
    total = fold_blocks(start_sum, (group_keys,), add_exp)
    log_total = jnp.log(total + jnp.sum(jnp.where(valid, jnp.exp(partner_logits), 0.0), axis=1))
    own_logits = SCALE * jnp.sum(
        query_rows.astype(jnp.float32) * key_rows.astype(jnp.float32), axis=1
    )
    loss = log_total - inverse * (
        own_logits + jnp.sum(jnp.where(valid, partner_logits, 0.0), axis=1)
    )
    partner_weights = jnp.where(
        valid, jnp.exp(partner_logits - log_total[:, None]) - inverse[:, None], 0.0
    ).astype(jnp.bfloat16)

    def add_grad(summed, block, offset):
        piece = block[0]
        scores = SCALE * jnp.dot(query_rows, piece.T, preferred_element_type=jnp.float32)
        columns = offset + jnp.arange(piece.shape[0], dtype=jnp.int32)
        target = jnp.where(mine[:, None] == columns[None, :], inverse[:, None], 0.0)
        weights = (jnp.exp(scores - log_total[:, None]) - target).astype(jnp.bfloat16)
        return summed + jnp.dot(weights, piece, preferred_element_type=jnp.float32)

    empty = jnp.zeros((anchors, width), jnp.float32)
    summed_q = fold_blocks(empty, (group_keys,), add_grad)
    grad_unit_q = SCALE * (
        summed_q
        + jnp.einsum(
            "ap,apd->ad", partner_weights, partner_keys, preferred_element_type=jnp.float32
        )
    )
    grad_queries = back_unit(unit_q, norm_q, grad_unit_q)
    all_log_total, all_inverse = (
        lax.all_gather(log_total, "loop", axis=0, tiled=True),
        lax.all_gather(inverse, "loop", axis=0, tiled=True),
    )

    def add_key_grad(summed, block, offset):
        piece = block[0]
        number = piece.shape[0]
        scores = SCALE * jnp.dot(piece, key_rows.T, preferred_element_type=jnp.float32)
        piece_log = lax.dynamic_slice_in_dim(all_log_total, offset, number)
        piece_inverse = lax.dynamic_slice_in_dim(all_inverse, offset, number)
        row_ids = offset + jnp.arange(number, dtype=jnp.int32)
        target = jnp.where(row_ids[:, None] == mine[None, :], piece_inverse[:, None], 0.0)
        weights = (jnp.exp(scores - piece_log[:, None]) - target).astype(jnp.bfloat16)
        return summed + lax.dot_general(
            weights, piece, (((0,), (0,)), ((), ())), preferred_element_type=jnp.float32
        )

    summed_k = fold_blocks(
        empty, (lax.all_gather(query_rows, "loop", axis=0, tiled=True),), add_key_grad
    )
    slot_weights = (
        jnp.zeros((sky_count * bucket,), jnp.bfloat16)
        .at[slot_index]
        .set(partner_weights.reshape(-1))
    )
    got_rows, got_weights = (
        lax.all_to_all(
            outgoing.reshape(sky_count, bucket, width),
            "sky",
            split_axis=0,
            concat_axis=0,
            tiled=True,
        ),
        lax.all_to_all(
            slot_weights.reshape(sky_count, bucket), "sky", split_axis=0, concat_axis=0, tiled=True
        ),
    )
    back_rows = got_rows.reshape(-1, width)
    back_weights = got_weights.reshape(-1)
    partner_grad = jax.ops.segment_sum(
        back_weights.astype(jnp.float32)[:, None] * back_rows.astype(jnp.float32),
        wanted,
        num_segments=anchors,
    )
    grad_keys = back_unit(unit_k, norm_k, SCALE * (summed_k + partner_grad))
    return (loss, grad_queries, grad_keys)


def solution(mesh):
    in_specs = (
        P(("sky", "loop"), None),
        P(("sky", "loop"), None),
        P(("sky", "loop"), None),
        P(("sky", "loop"), None),
        P(("sky", "loop")),
    )
    out_specs = (P(("sky", "loop")), P(("sky", "loop"), None), P(("sky", "loop"), None))
    return jax.shard_map(shards, mesh=mesh, in_specs=in_specs, out_specs=out_specs, check_vma=False)
```

profile of v0, /device:TPU:1, one launch (start us, length us, event | category | flops | bytes accessed | tf_op | source)
XLA Modules:
  0.0 580.1 jit_solution(7854657634066408081)
XLA Ops:
  9.6 2.9 multiply_reduce_fusion.2
  13.6 9.2 %reduce-window.6 = s32[32,24,128]{2,1,0:T(8,128)S(1)} reduce-window(s32[32,24,128]{2,1,0:T(8,128)S(1)} %fusion.55, s32[]{:T(128)} %constant.48.clone.1), window={size=1x1x128 pad=0_0x0_0x127_0}, to_apply=%region_5.6 | reduce-window | flops 12484608 | bytes 786436 | tf_op jit(solution)/shard_map/reduce-window
  24.8 11.8 %scatter_custom_fusion = s32[6144]{0:T(1024)S(1)} fusion(s32[3072]{0:T(1024)S(1)} %bitcast.109, s32[3072]{0:T(1024)S(1)} %reshape.223, s32[]{:T(128)} %constant.48.clone.1), kind=kCustom, calls=%fused_computation.91 | custom fusion | bytes 24580 | tf_op jit(solution)/shard_map/scatter | solution.py:53
  36.7 17.5 %all_to_all.29 = s32[32,1,192]{2,1,0:T(1,128)S(1)} all-to-all(s32[32,1,192]{2,1,0:T(1,128)S(1)} %all_to_all.18), channel_id=1, replica_groups=mesh['sky'=32,'loop'=8] {'sky'}, dimensions={0} | all-to-all | bytes 49152 | tf_op jit(solution)/shard_map/all_to_all | solution.py:55
  55.5 24.7 %gather_fusion = bf16[6144,256]{1,0:T(8,128)(2,1)S(1)} fusion(bf16[768,256]{1,0:T(8,128)(2,1)S(1)} %copy-done, s32[6144]{0:T(1024)} %broadcast_clamp_fusion), kind=kCustom, calls=%fused_computation | custom fusion | bytes 6316032 | tf_op jit(solution)/shard_map/jit(_take)/gather | solution.py:59
  80.9 2.7 broadcast_select_fusion
  83.6 4.3 all-to-all-start.1
  93.1 2.5 broadcast_in_dim.101
  95.6 3.5 reshape.239
  99.1 16.1 %scatter_custom_fusion.2 = bf16[6144,256]{1,0:T(8,128)(2,1)} fusion(s32[3072]{0:T(1024)} %bitcast.110, bf16[3072,256]{1,0:T(8,128)(2,1)} %reshape.239, bf16[]{:T(256)} %constant.95.clone.1), kind=kCustom, calls=%fused_computation.50 | custom fusion | bytes 3146240 | tf_op jit(solution)/shard_map/scatter | solution.py:69
  118.6 18.6 %while.33 = (s32[]{:T(128)}, f32[768]{0:T(1024)S(1)}, bf16[12,512,256]{2,1,0:T(8,128)(2,1)}, bf16[768,256]{1,0:T(8,128)(2,1)}, s32[]{:T(128)}, /*index=5*/s32[]{:T(128)}) while((s32[]{:T(128)}, f32[768]{0:T(1024)S(1)}, bf16[12,512,256]{2,1,0:T(8,128)(2,1)}, bf16[768,256]{1,0:T(8,128)(2,1)}, s32[]{:T(128)}, ...), condition=%wide.region_4.5_spmd.clone, body=%wide.region_2.4_spmd.clone.sunk | while | flops 202113792 | bytes 667739 | solution.py:30
  137.2 69.8 %all-to-all-done.1 = bf16[32,192,256]{2,1,0:T(8,128)(2,1)S(1)} async-done(((bf16[32,192,256]{2,1,0:T(8,128)(2,1)}), bf16[32,192,256]{2,1,0:T(8,128)(2,1)S(1)}, u32[]{:S(2)}, u32[]{:S(2)}) %all-to-all-start.1) | async-done | bytes 3145760 | tf_op jit(solution)/shard_map/all_to_all | solution.py:60
  207.1 14.0 %gather_fusion.1 = bf16[3072,256]{1,0:T(8,128)(2,1)} fusion(bf16[6144,256]{1,0:T(8,128)(2,1)S(1)} %bitcast.95, s32[3072]{0:T(1024)} %broadcast_clamp_fusion.1), kind=kCustom, calls=%fused_computation.1 | custom fusion | bytes 3158016 | tf_op jit(solution)/shard_map/jit(_take)/gather | solution.py:63
  221.0 2.4 gather.15
  223.5 6.5 %fusion.45 = f32[768,1,4]{2,1,0:T(1,128)S(1)} fusion(bf16[768,4,256]{2,1,0:T(4,128)(2,1)S(1)} %gather.15, pred[768,4]{1,0:T(8,128)(4,1)S(1)} %copy-done.12, bf16[768,256,1]{1,0,2:T(8,128)(2,1)S(1)} %bitcast.101), kind=kOutput, calls=%fused_computation.54 | convolution fusion | flops 2359296 | bytes 1981440 | tf_op jit(solution)/shard_map/apd,ad->ap/dot_general | solution.py:71
  231.9 3.7 fusion.44
  235.8 21.7 %scatter_custom_fusion.1 = bf16[6144]{0:T(1024)(128)(2,1)S(1)} fusion(s32[3072]{0:T(1024)} %bitcast.112, bf16[3072]{0:T(1024)(128)(2,1)S(1)} %reshape.231, bf16[]{:T(256)} %constant.95.clone.1), kind=kCustom, calls=%fused_computation.95 | custom fusion | bytes 12800 | tf_op jit(solution)/shard_map/scatter | solution.py:134
  258.2 6.6 %all-to-all-start.2 = ((bf16[32,1,192]{2,1,0:T(2,128)(2,1)}), bf16[32,1,192]{2,1,0:T(2,128)(2,1)S(1)}, u32[]{:S(2)}, u32[]{:S(2)}) async-start(bf16[32,1,192]{2,1,0:T(2,128)(2,1)} %all_to_all.24), calls=%async_computation.2 | async-start | bytes 65536 | tf_op jit(solution)/shard_map/all_to_all | solution.py:144
  264.9 49.0 %while.34 = (s32[]{:T(128)}, f32[768,256]{1,0:T(8,128)S(1)}, bf16[12,512,256]{2,1,0:T(8,128)(2,1)}, bf16[768,256]{1,0:T(8,128)(2,1)S(1)}, f32[768]{0:T(1024)S(1)...) while((s32[]{:T(128)}, f32[768,256]{1,0:T(8,128)S(1)}, ...), condition=%wide.region_13.14_spmd.clone, body=%wide.region_12.13_spmd.clone.sunk | while | flops 405406976 | bytes 2508426 | solution.py:30
  266.9 2.1 fusion.86
  270.9 2.1 fusion.86
  275.0 2.1 fusion.86
  279.1 2.1 fusion.86
  283.2 2.1 fusion.86
  287.2 2.1 fusion.86
  291.3 2.1 fusion.86
  295.4 2.1 fusion.86
  299.5 2.1 fusion.86
  303.6 2.1 fusion.86
  307.6 2.1 fusion.86
  311.7 2.2 fusion.86
  315.5 39.1 %all-gather = f32[8,1,768]{2,1,0:T(1,128)} all-gather(f32[1,1,768]{2,1,0:T(1,128)S(1)} %reshape.252), channel_id=1, replica_groups=mesh['sky'=32,'loop'=8] {'loop'}, dimensions={0}, use_global_device_ids=true | all-gather | bytes 27648 | tf_op jit(solution)/shard_map/all_gather | solution.py:111
  354.6 38.8 %all-gather.1 = f32[8,1,768]{2,1,0:T(1,128)} all-gather(f32[1,1,768]{2,1,0:T(1,128)S(1)} %reshape.254), channel_id=1, replica_groups=mesh['sky'=32,'loop'=8] {'loop'}, dimensions={0}, use_global_device_ids=true | all-gather | bytes 27648 | tf_op jit(solution)/shard_map/all_gather | solution.py:112
  394.1 20.4 %all-to-all-start.3 = ((bf16[32,192,256]{2,1,0:T(8,128)(2,1)}), bf16[32,192,256]{2,1,0:T(8,128)(2,1)S(1)}, u32[]{:S(2)}, u32[]{:S(2)}) async-start(bf16[32,192,256]{2,1,0:T(8,128)(2,1)} %bitcast.17), calls=%async_computation.3 | async-start | bytes 6291456 | tf_op jit(solution)/shard_map/all_to_all | solution.py:137
  414.5 112.3 %while.35 = (s32[]{:T(128)}, f32[768,256]{1,0:T(8,128)}, bf16[12,512,256]{2,1,0:T(8,128)(2,1)}, bf16[768,256]{1,0:T(8,128)(2,1)S(1)}, s32[12]{0:T(128)}, /*index...) while((s32[]{:T(128)}, f32[768,256]{1,0:T(8,128)}, ...), condition=%wide.region_16.17_spmd.clone, body=%wide.region_15.16_spmd.clone.sunk | while | flops 405406976 | bytes 2514620 | solution.py:30
  420.8 2.9 fusion.90
  429.9 3.2 fusion.90
  439.3 3.2 fusion.90
  448.7 3.2 fusion.90
  458.1 3.2 fusion.90
  467.4 3.2 fusion.90
  476.8 3.2 fusion.90
  486.2 3.2 fusion.90
  495.6 3.2 fusion.90
  505.0 3.2 fusion.90
  514.3 3.2 fusion.90
  523.7 3.2 fusion.90
  528.4 42.2 %scatter_custom_fusion.3 = f32[768,256]{1,0:T(8,128)} fusion(f32[768,256]{1,0:T(8,128)} %get-tuple-element.111, s32[6144]{0:T(1024)} %reshape.245, bf16[6144,256]{1,0:T(8,128)(2,1)S(1)} %bitcast.97, f32[6144]{0:T(1024)} %reshape.201), kind=kCustom, calls=%fused_computation.47 | custom fusion | flops 4718592 | bytes 3956736 | tf_op jit(solution)/shard_map/scatter-add | solution.py:150
  (214 shorter events, 116.2 us)
Async XLA Ops:
  7.2 5.3 copy-start.11
  7.2 111.4 %all-gather.5.cloned.1.call-start = ((), (), s32[]{:S(2)}) async-start(), calls=%async_computation.4 | async-start | bytes 3538944 | tf_op jit(solution)/shard_map/all_gather | solution.py:80
  9.6 2.9 copy-start.13
  13.1 10.3 %copy-start.18 = (s32[768,4]{0,1:T(4,128)S(1)}, s32[768,4]{0,1:T(4,128)}, u32[]{:S(2)}) copy-start(s32[768,4]{0,1:T(4,128)} %param.14) | copy-start | bytes 36868
  23.0 32.5 %copy-start = (bf16[768,256]{1,0:T(8,128)(2,1)S(1)}, bf16[768,256]{1,0:T(8,128)(2,1)}, u32[]{:S(2)}) copy-start(bf16[768,256]{1,0:T(8,128)(2,1)} %get-tuple-element.411) | copy-start | bytes 1179652
  24.2 0.6 copy-start.16
  54.2 0.6 copy-start.9
  54.3 0.6 copy-start.8
  83.6 123.5 %all-to-all-start.1 = ((bf16[32,192,256]{2,1,0:T(8,128)(2,1)}), bf16[32,192,256]{2,1,0:T(8,128)(2,1)S(1)}, u32[]{:S(2)}, u32[]{:S(2)}) async-start(bf16[32,192,256]{2,1,0:T(8,128)(2,1)} %broadcast_select_fusion), calls=%async_computation.1 | async-start | bytes 6291456 | tf_op jit(solution)/shard_map/all_to_all | solution.py:60
  87.9 326.7 %all-gather.7.cloned.1.call-start = ((), (), s32[]{:S(2)}) async-start(), calls=%async_computation.5 | async-start | bytes 3538944 | tf_op jit(solution)/shard_map/all_gather | solution.py:129
  221.0 2.4 copy-start.3
  221.0 2.4 copy-start.12
  223.4 6.6 %copy-start.6 = (bf16[768,4,256]{2,1,0:T(4,128)(2,1)}, bf16[768,4,256]{2,1,0:T(4,128)(2,1)S(1)}, u32[]{:S(2)}) copy-start(bf16[768,4,256]{2,1,0:T(4,128)(2,1)S(1)} %gather.15) | copy-start | bytes 4718596
  223.5 6.6 %copy-start.15 = (s32[768]{0:T(1024)S(1)}, s32[768]{0:T(1024)}, u32[]{:S(2)}) copy-start(s32[768]{0:T(1024)} %param.15) | copy-start | bytes 9220
  223.5 7.0 %copy-start.17 = (f32[768]{0:T(1024)S(1)}, f32[768]{0:T(1024)}, u32[]{:S(2)}) copy-start(f32[768]{0:T(1024)} %get-tuple-element.231) | copy-start | bytes 9220
  230.1 1.8 copy-start.7
  231.9 33.0 %copy-start.5 = (f32[768,256]{1,0:T(8,128)S(1)}, f32[768,256]{1,0:T(8,128)}, u32[]{:S(2)}) copy-start(f32[768,256]{1,0:T(8,128)} %custom-call.1) | copy-start | bytes 2359300
  258.2 135.2 %all-to-all-start.2 = ((bf16[32,1,192]{2,1,0:T(2,128)(2,1)}), bf16[32,1,192]{2,1,0:T(2,128)(2,1)S(1)}, u32[]{:S(2)}, u32[]{:S(2)}) async-start(bf16[32,1,192]{2,1,0:T(2,128)(2,1)} %all_to_all.24), calls=%async_computation.2 | async-start | bytes 65536 | tf_op jit(solution)/shard_map/all_to_all | solution.py:144
  264.9 49.0 %copy-start.2 = (bf16[768,256]{1,0:T(8,128)(2,1)S(1)}, bf16[768,256]{1,0:T(8,128)(2,1)}, u32[]{:S(2)}) copy-start(bf16[768,256]{1,0:T(8,128)(2,1)} %param.11) | copy-start | bytes 1179652
  264.9 49.0 %copy-start.14 = (f32[768]{0:T(1024)S(1)}, f32[768]{0:T(1024)}, u32[]{:S(2)}) copy-start(f32[768]{0:T(1024)} %copy-done.13) | copy-start | bytes 9220
  393.4 0.6 copy-start.10
  394.1 134.3 %all-to-all-start.3 = ((bf16[32,192,256]{2,1,0:T(8,128)(2,1)}), bf16[32,192,256]{2,1,0:T(8,128)(2,1)S(1)}, u32[]{:S(2)}, u32[]{:S(2)}) async-start(bf16[32,192,256]{2,1,0:T(8,128)(2,1)} %bitcast.17), calls=%async_computation.3 | async-start | bytes 6291456 | tf_op jit(solution)/shard_map/all_to_all | solution.py:137
  528.4 42.2 %copy-start.1 = (bf16[768,256]{1,0:T(8,128)(2,1)S(1)}, bf16[768,256]{1,0:T(8,128)(2,1)}, u32[]{:S(2)}) copy-start(bf16[768,256]{1,0:T(8,128)(2,1)} %param.12) | copy-start | bytes 1179652
  570.6 1.6 copy-start.4
Sparse Core Ops, SparseCore 0:
  12.6 90.2 all-gather.4
  105.5 85.9 all-gather.6
where the time goes:
time: 584 us; the launch traced here: 580 us
  local copies, waits for them, and re-layouts  164 us (28%)
  blocking collectives  95.4 us (16%)
  matrix products  91.6 us (16%)
  other arithmetic  86.9 us (15%)
  waiting for transfers between devices  70.6 us (12%)
  starting transfers between devices  31.4 us (5%)
  loops' own time  25.9 us (4%)
  between operations  14.5 us (2%)
    all_to_all x1, waiting for transfers between devices, shards(): lax.all_to_all(replies.reshape(sky_count, bucket, width), 'sky', split_ax...  69.8 us
    scatter-add x1, other arithmetic, shards(): jax.ops.segment_sum(back_weights.astype(jnp.float32)[:, None] * back_rows...  42.2 us
    all_gather x1, blocking collectives, shards(): lax.all_gather(log_total, 'loop', axis=0, tiled=True)  39.1 us
    all_gather x1, blocking collectives, shards(): lax.all_gather(inverse, 'loop', axis=0, tiled=True)  38.8 us
    dot_general x12, matrix products, add_key_grad(): lax.dot_general(weights, piece, (((0,), (0,)), ((), ())), preferred_eleme...  37.6 us
    dynamic_slice x24, local copies, waits for them, and re-layouts, fold_blocks(): result, unused = lax.scan(one_turn, carry, (split, offsets))  30.9 us
    another operation x3, loops' own time, fold_blocks(): result, unused = lax.scan(one_turn, carry, (split, offsets))  25.9 us
    dot_general x12, matrix products, add_grad(): return summed + jnp.dot(weights, piece, preferred_element_type=jnp.float32)  25.6 us
  transfers between devices with their start and end apart: 5, of which 1 were waited for; matrix products, arithmetic and copies ran while one was open for 50% of the time, Pallas kernels for 0%

commit v1 on v0

--- a/solution.py
+++ b/solution.py
@@ -107,9 +107,18 @@
         )
     )
     grad_queries = back_unit(unit_q, norm_q, grad_unit_q)
+    reach_slot = lambda array_in, peer_axis: jnp.concatenate(
+        lax.all_to_all(
+            jnp.stack(lax.axis_size(peer_axis) * [array_in], axis=0),
+            peer_axis,
+            split_axis=0,
+            concat_axis=0,
+        ),
+        axis=0,
+    )
     all_log_total, all_inverse = (
         lax.all_gather(log_total, "loop", axis=0, tiled=True),
-        lax.all_gather(inverse, "loop", axis=0, tiled=True),
+        reach_slot(inverse, "loop"),
     )
 
     def add_key_grad(summed, block, offset):

time: 584 us -> 548 us (0.938)
  blocking collectives: 95.4 us -> 56.9 us
    all_gather x1 -> x0, blocking collectives: 38.8 us -> none  [shards(): lax.all_gather(inverse, 'loop', axis=0, tiled=True)]
    all_to_all x1, starting transfers between devices: 20.4 us -> 14 us  [shards(): lax.all_to_all(outgoing.reshape(sky_count, bucket, width), 'sky', split_a...]
    all_to_all x0 -> x1, starting transfers between devices: none -> 6.13 us  [shards(): lax.all_to_all(jnp.stack(lax.axis_size(peer_axis) * [array_in], axis=0),...]
  transfers between devices with their start and end apart: 5 -> 6, of which waited for: 1 -> 1; matrix products, arithmetic and copies ran while one was open for 50% -> 54% of each run, Pallas kernels for 0% -> 0%
where the time goes in v1:
time: 548 us; the launch traced here: 543 us
  local copies, waits for them, and re-layouts  165 us (30%)
  matrix products  91.6 us (17%)
  other arithmetic  87.5 us (16%)
  waiting for transfers between devices  70.6 us (13%)
  blocking collectives  56.9 us (10%)
  starting transfers between devices  31.1 us (6%)
  loops' own time  25.9 us (5%)
  between operations  14.5 us (3%)
    all_to_all x1, waiting for transfers between devices, shards(): lax.all_to_all(replies.reshape(sky_count, bucket, width), 'sky', split_ax...  69.8 us
    scatter-add x1, other arithmetic, shards(): jax.ops.segment_sum(back_weights.astype(jnp.float32)[:, None] * back_rows...  42.2 us
    all_gather x1, blocking collectives, shards(): lax.all_gather(log_total, 'loop', axis=0, tiled=True)  39.4 us
    dot_general x12, matrix products, add_key_grad(): lax.dot_general(weights, piece, (((0,), (0,)), ((), ())), preferred_eleme...  37.6 us
    dynamic_slice x24, local copies, waits for them, and re-layouts, fold_blocks(): result, unused = lax.scan(one_turn, carry, (split, offsets))  30.9 us
    another operation x3, loops' own time, fold_blocks(): result, unused = lax.scan(one_turn, carry, (split, offsets))  25.9 us
    dot_general x12, matrix products, add_grad(): return summed + jnp.dot(weights, piece, preferred_element_type=jnp.float32)  25.6 us
    gather x1, local copies, waits for them, and re-layouts, shards(): replies = jnp.take(key_rows, wanted, axis=0)  24.7 us
  transfers between devices with their start and end apart: 6, of which 1 were waited for; matrix products, arithmetic and copies ran while one was open for 54% of the time, Pallas kernels for 0%

profile of v1, /device:TPU:1, one launch (start us, length us, event | category | flops | bytes accessed | tf_op | source)
XLA Modules:
  0.0 543.3 jit_solution(7137594246318376062)
XLA Ops:
  9.6 2.9 multiply_reduce_fusion.2
  13.6 9.2 %reduce-window.6 = s32[32,24,128]{2,1,0:T(8,128)S(1)} reduce-window(s32[32,24,128]{2,1,0:T(8,128)S(1)} %fusion.55, s32[]{:T(128)} %constant.48.clone.1), window={size=1x1x128 pad=0_0x0_0x127_0}, to_apply=%region_5.6 | reduce-window | flops 12484608 | bytes 786436 | tf_op jit(solution)/shard_map/reduce-window
  24.8 11.8 %scatter_custom_fusion = s32[6144]{0:T(1024)S(1)} fusion(s32[3072]{0:T(1024)S(1)} %bitcast.109, s32[3072]{0:T(1024)S(1)} %reshape.235, s32[]{:T(128)} %constant.48.clone.1), kind=kCustom, calls=%fused_computation.91 | custom fusion | bytes 24580 | tf_op jit(solution)/shard_map/scatter | solution.py:53
  36.7 17.5 %all_to_all.35 = s32[32,1,192]{2,1,0:T(1,128)S(1)} all-to-all(s32[32,1,192]{2,1,0:T(1,128)S(1)} %all_to_all.22), channel_id=1, replica_groups=mesh['sky'=32,'loop'=8] {'sky'}, dimensions={0} | all-to-all | bytes 49152 | tf_op jit(solution)/shard_map/all_to_all | solution.py:55
  55.5 24.7 %gather_fusion = bf16[6144,256]{1,0:T(8,128)(2,1)S(1)} fusion(bf16[768,256]{1,0:T(8,128)(2,1)S(1)} %copy-done, s32[6144]{0:T(1024)} %broadcast_clamp_fusion), kind=kCustom, calls=%fused_computation | custom fusion | bytes 6316032 | tf_op jit(solution)/shard_map/jit(_take)/gather | solution.py:59
  80.9 2.7 broadcast_select_fusion
  83.6 4.3 all-to-all-start.1
  93.1 2.5 broadcast_in_dim.101
  95.6 3.5 reshape.251
  99.1 16.1 %scatter_custom_fusion.2 = bf16[6144,256]{1,0:T(8,128)(2,1)} fusion(s32[3072]{0:T(1024)} %bitcast.110, bf16[3072,256]{1,0:T(8,128)(2,1)} %reshape.251, bf16[]{:T(256)} %constant.95.clone.1), kind=kCustom, calls=%fused_computation.50 | custom fusion | bytes 3146240 | tf_op jit(solution)/shard_map/scatter | solution.py:69
  118.6 18.6 %while.33 = (s32[]{:T(128)}, f32[768]{0:T(1024)S(1)}, bf16[12,512,256]{2,1,0:T(8,128)(2,1)}, bf16[768,256]{1,0:T(8,128)(2,1)}, s32[]{:T(128)}, /*index=5*/s32[]{:T(128)}) while((s32[]{:T(128)}, f32[768]{0:T(1024)S(1)}, bf16[12,512,256]{2,1,0:T(8,128)(2,1)}, bf16[768,256]{1,0:T(8,128)(2,1)}, s32[]{:T(128)}, ...), condition=%wide.region_4.5_spmd.clone, body=%wide.region_2.4_spmd.clone.sunk | while | flops 202113792 | bytes 667739 | solution.py:30
  137.2 69.8 %all-to-all-done.1 = bf16[32,192,256]{2,1,0:T(8,128)(2,1)S(1)} async-done(((bf16[32,192,256]{2,1,0:T(8,128)(2,1)}), bf16[32,192,256]{2,1,0:T(8,128)(2,1)S(1)}, u32[]{:S(2)}, u32[]{:S(2)}) %all-to-all-start.1) | async-done | bytes 3145760 | tf_op jit(solution)/shard_map/all_to_all | solution.py:60
  207.1 14.0 %gather_fusion.1 = bf16[3072,256]{1,0:T(8,128)(2,1)} fusion(bf16[6144,256]{1,0:T(8,128)(2,1)S(1)} %bitcast.95, s32[3072]{0:T(1024)} %broadcast_clamp_fusion.1), kind=kCustom, calls=%fused_computation.1 | custom fusion | bytes 3158016 | tf_op jit(solution)/shard_map/jit(_take)/gather | solution.py:63
  221.0 2.4 gather.15
  223.5 6.5 %fusion.45 = f32[768,1,4]{2,1,0:T(1,128)S(1)} fusion(bf16[768,4,256]{2,1,0:T(4,128)(2,1)S(1)} %gather.15, pred[768,4]{1,0:T(8,128)(4,1)S(1)} %copy-done.12, bf16[768,256,1]{1,0,2:T(8,128)(2,1)S(1)} %bitcast.101), kind=kOutput, calls=%fused_computation.54 | convolution fusion | flops 2359296 | bytes 1981440 | tf_op jit(solution)/shard_map/apd,ad->ap/dot_general | solution.py:71
  231.9 3.7 fusion.44
  235.8 21.7 %scatter_custom_fusion.1 = bf16[6144]{0:T(1024)(128)(2,1)S(1)} fusion(s32[3072]{0:T(1024)} %bitcast.112, bf16[3072]{0:T(1024)(128)(2,1)S(1)} %reshape.243, bf16[]{:T(256)} %constant.95.clone.1), kind=kCustom, calls=%fused_computation.95 | custom fusion | bytes 12800 | tf_op jit(solution)/shard_map/scatter | solution.py:143
  258.2 6.6 %all-to-all-start.3 = ((bf16[32,1,192]{2,1,0:T(2,128)(2,1)}), bf16[32,1,192]{2,1,0:T(2,128)(2,1)S(1)}, u32[]{:S(2)}, u32[]{:S(2)}) async-start(bf16[32,1,192]{2,1,0:T(2,128)(2,1)} %all_to_all.29), calls=%async_computation.3 | async-start | bytes 65536 | tf_op jit(solution)/shard_map/all_to_all | solution.py:153
  264.9 49.0 %while.34 = (s32[]{:T(128)}, f32[768,256]{1,0:T(8,128)S(1)}, bf16[12,512,256]{2,1,0:T(8,128)(2,1)}, bf16[768,256]{1,0:T(8,128)(2,1)S(1)}, f32[768]{0:T(1024)S(1)...) while((s32[]{:T(128)}, f32[768,256]{1,0:T(8,128)S(1)}, ...), condition=%wide.region_13.14_spmd.clone, body=%wide.region_12.13_spmd.clone.sunk | while | flops 405406976 | bytes 2508426 | solution.py:30
  266.9 2.1 fusion.86
  270.9 2.1 fusion.86
  275.0 2.1 fusion.86
  279.1 2.1 fusion.86
  283.2 2.1 fusion.86
  287.3 2.1 fusion.86
  291.3 2.1 fusion.86
  295.4 2.1 fusion.86
  299.5 2.1 fusion.86
  303.6 2.1 fusion.86
  307.6 2.1 fusion.86
  311.7 2.2 fusion.86
  315.0 6.1 %all-to-all-start.2 = ((f32[8,1,768]{2,1,0:T(1,128)}), f32[8,1,768]{2,1,0:T(1,128)S(1)}, u32[]{:S(2)}, u32[]{:S(2)}) async-start(f32[8,1,768]{2,1,0:T(1,128)} %stack.2), calls=%async_computation.2 | async-start | bytes 49152 | tf_op jit(solution)/shard_map/all_to_all | solution.py:111
  322.3 39.4 %all-gather = f32[8,1,768]{2,1,0:T(1,128)} all-gather(f32[1,1,768]{2,1,0:T(1,128)S(1)} %reshape.264), channel_id=1, replica_groups=mesh['sky'=32,'loop'=8] {'loop'}, dimensions={0}, use_global_device_ids=true | all-gather | bytes 27648 | tf_op jit(solution)/shard_map/all_gather | solution.py:120
  362.3 14.0 %all-to-all-start.4 = ((bf16[32,192,256]{2,1,0:T(8,128)(2,1)}), bf16[32,192,256]{2,1,0:T(8,128)(2,1)S(1)}, u32[]{:S(2)}, u32[]{:S(2)}) async-start(bf16[32,192,256]{2,1,0:T(8,128)(2,1)} %bitcast.17), calls=%async_computation.4 | async-start | bytes 6291456 | tf_op jit(solution)/shard_map/all_to_all | solution.py:146
  379.2 112.3 %while.35 = (s32[]{:T(128)}, f32[768,256]{1,0:T(8,128)}, bf16[12,512,256]{2,1,0:T(8,128)(2,1)}, bf16[768,256]{1,0:T(8,128)(2,1)S(1)}, s32[12]{0:T(128)}, /*index...) while((s32[]{:T(128)}, f32[768,256]{1,0:T(8,128)}, ...), condition=%wide.region_16.17_spmd.clone, body=%wide.region_15.16_spmd.clone.sunk | while | flops 405406976 | bytes 2514620 | solution.py:30
  385.5 2.9 fusion.90
  394.6 3.2 fusion.90
  404.0 3.2 fusion.90
  413.4 3.2 fusion.90
  422.7 3.2 fusion.90
  432.1 3.2 fusion.90
  441.5 3.2 fusion.90
  450.9 3.2 fusion.90
  460.3 3.2 fusion.90
  469.7 3.2 fusion.90
  479.0 3.2 fusion.90
  488.4 3.2 fusion.90
  491.5 42.2 %scatter_custom_fusion.3 = f32[768,256]{1,0:T(8,128)} fusion(f32[768,256]{1,0:T(8,128)} %get-tuple-element.111, s32[6144]{0:T(1024)} %reshape.257, bf16[6144,256]{1,0:T(8,128)(2,1)S(1)} %bitcast.97, f32[6144]{0:T(1024)} %reshape.213), kind=kCustom, calls=%fused_computation.47 | custom fusion | flops 4718592 | bytes 3956736 | tf_op jit(solution)/shard_map/scatter-add | solution.py:159
  (217 shorter events, 118.1 us)
Async XLA Ops:
  7.2 5.3 copy-start.11
  7.2 111.4 %all-gather.4.cloned.1.call-start = ((), (), s32[]{:S(2)}) async-start(), calls=%async_computation.5 | async-start | bytes 3538944 | tf_op jit(solution)/shard_map/all_gather | solution.py:80
  9.6 2.9 copy-start.13
  13.1 10.3 %copy-start.19 = (s32[768,4]{0,1:T(4,128)S(1)}, s32[768,4]{0,1:T(4,128)}, u32[]{:S(2)}) copy-start(s32[768,4]{0,1:T(4,128)} %param.14) | copy-start | bytes 36868
  23.0 32.5 %copy-start = (bf16[768,256]{1,0:T(8,128)(2,1)S(1)}, bf16[768,256]{1,0:T(8,128)(2,1)}, u32[]{:S(2)}) copy-start(bf16[768,256]{1,0:T(8,128)(2,1)} %get-tuple-element.411) | copy-start | bytes 1179652
  24.2 0.6 copy-start.17
  54.2 0.6 copy-start.9
  54.3 0.6 copy-start.8
  83.6 123.5 %all-to-all-start.1 = ((bf16[32,192,256]{2,1,0:T(8,128)(2,1)}), bf16[32,192,256]{2,1,0:T(8,128)(2,1)S(1)}, u32[]{:S(2)}, u32[]{:S(2)}) async-start(bf16[32,192,256]{2,1,0:T(8,128)(2,1)} %broadcast_select_fusion), calls=%async_computation.1 | async-start | bytes 6291456 | tf_op jit(solution)/shard_map/all_to_all | solution.py:60
  87.9 291.4 %all-gather.6.cloned.1.call-start = ((), (), s32[]{:S(2)}) async-start(), calls=%async_computation.6 | async-start | bytes 3538944 | tf_op jit(solution)/shard_map/all_gather | solution.py:138
  221.0 2.4 copy-start.3
  221.0 2.4 copy-start.12
  223.4 6.6 %copy-start.6 = (bf16[768,4,256]{2,1,0:T(4,128)(2,1)}, bf16[768,4,256]{2,1,0:T(4,128)(2,1)S(1)}, u32[]{:S(2)}) copy-start(bf16[768,4,256]{2,1,0:T(4,128)(2,1)S(1)} %gather.15) | copy-start | bytes 4718596
  223.5 6.6 %copy-start.15 = (s32[768]{0:T(1024)S(1)}, s32[768]{0:T(1024)}, u32[]{:S(2)}) copy-start(s32[768]{0:T(1024)} %param.15) | copy-start | bytes 9220
  223.5 7.0 %copy-start.18 = (f32[768]{0:T(1024)S(1)}, f32[768]{0:T(1024)}, u32[]{:S(2)}) copy-start(f32[768]{0:T(1024)} %get-tuple-element.231) | copy-start | bytes 9220
  230.1 1.8 copy-start.7
  231.9 33.0 %copy-start.5 = (f32[768,256]{1,0:T(8,128)S(1)}, f32[768,256]{1,0:T(8,128)}, u32[]{:S(2)}) copy-start(f32[768,256]{1,0:T(8,128)} %custom-call.1) | copy-start | bytes 2359300
  258.2 56.1 %all-to-all-start.3 = ((bf16[32,1,192]{2,1,0:T(2,128)(2,1)}), bf16[32,1,192]{2,1,0:T(2,128)(2,1)S(1)}, u32[]{:S(2)}, u32[]{:S(2)}) async-start(bf16[32,1,192]{2,1,0:T(2,128)(2,1)} %all_to_all.29), calls=%async_computation.3 | async-start | bytes 65536 | tf_op jit(solution)/shard_map/all_to_all | solution.py:153
  264.9 49.0 %copy-start.2 = (bf16[768,256]{1,0:T(8,128)(2,1)S(1)}, bf16[768,256]{1,0:T(8,128)(2,1)}, u32[]{:S(2)}) copy-start(bf16[768,256]{1,0:T(8,128)(2,1)} %param.11) | copy-start | bytes 1179652
  264.9 49.0 %copy-start.14 = (f32[768]{0:T(1024)S(1)}, f32[768]{0:T(1024)}, u32[]{:S(2)}) copy-start(f32[768]{0:T(1024)} %copy-done.13) | copy-start | bytes 9220
  314.4 47.3 %copy-start.10 = (bf16[32,1,192]{2,1,0:T(2,128)(2,1)}, bf16[32,1,192]{2,1,0:T(2,128)(2,1)S(1)}, u32[]{:S(2)}) copy-start(bf16[32,1,192]{2,1,0:T(2,128)(2,1)S(1)} %all-to-all-done.3) | copy-start | bytes 36868
  315.0 46.7 %all-to-all-start.2 = ((f32[8,1,768]{2,1,0:T(1,128)}), f32[8,1,768]{2,1,0:T(1,128)S(1)}, u32[]{:S(2)}, u32[]{:S(2)}) async-start(f32[8,1,768]{2,1,0:T(1,128)} %stack.2), calls=%async_computation.2 | async-start | bytes 49152 | tf_op jit(solution)/shard_map/all_to_all | solution.py:111
  361.7 0.6 copy-start.16
  362.3 129.3 %all-to-all-start.4 = ((bf16[32,192,256]{2,1,0:T(8,128)(2,1)}), bf16[32,192,256]{2,1,0:T(8,128)(2,1)S(1)}, u32[]{:S(2)}, u32[]{:S(2)}) async-start(bf16[32,192,256]{2,1,0:T(8,128)(2,1)} %bitcast.17), calls=%async_computation.4 | async-start | bytes 6291456 | tf_op jit(solution)/shard_map/all_to_all | solution.py:146
  491.5 42.2 %copy-start.1 = (bf16[768,256]{1,0:T(8,128)(2,1)S(1)}, bf16[768,256]{1,0:T(8,128)(2,1)}, u32[]{:S(2)}) copy-start(bf16[768,256]{1,0:T(8,128)(2,1)} %param.12) | copy-start | bytes 1179652
  533.7 1.6 copy-start.4
Sparse Core Ops, SparseCore 0:
  12.6 90.2 all-gather.3
  105.5 85.9 all-gather.5
